TPU v7x, 32 devices: a whole 2x2x4 slice. The times are simulated.
32 devices in a mesh: grp: 2 (over y), ja: 4 (over z), ia: 4 (over x, core).
Axes of the slice: x: 2, y: 2, z: 4, core: 2. Of those that a mesh axis runs over, the one named last changes fastest.
Arguments:
- pos_vel: float32 [6, 8192], P(None, ('grp', 'ja')), parts along dimension 1, may hold values from -6 to 6
- acc_jerk: float32 [6, 8192], P(None, ('grp', 'ja')), parts along dimension 1, may hold values from -6 to 6
- mass: float32 [8192], P(('grp', 'ja')), parts along dimension 0, may hold values from 7.324219e-05 to 0.0007324219
- age: float32 [8192], P(('grp', 'ja')), parts along dimension 0, may hold values from 0.125 to 0.5
- active_local: int32 [12288], P(('grp', 'ia')), parts along dimension 0, may hold values from 0 to 1023
- active_owner: int32 [12288], P(('grp', 'ia')), parts along dimension 0, may hold values from 0 to 3
Outputs:
- state: float32 [6, 12288], P(None, ('grp', 'ia')), parts along dimension 1
- forces: float32 [7, 12288], P(None, ('grp', 'ia')), parts along dimension 1
There are 2 independent parts, one for each index of `grp`. A program takes and returns all parts, laid end to end along the dimension named above; each array names one. Nothing has to cross between parts.
All inputs are finite; a program needn't handle non-finite values.
Results may differ from a plain program's by a relative error of at most 0.0003.
Values sent between devices are 32-bit elements; how exact they have to be, the bound alone decides.
No kernel may reach another device: no remote copies, remote signals or barrier semaphores. Data moves between devices by JAX's collectives and lax.ppermute only.
A program may use at most 64 MiB of HBM per device.

v0:
```python
import jax
import jax.numpy as jnp
from jax import lax
from jax.sharding import PartitionSpec as P

soften = 0.0004


def predict(pos_vel, acc_jerk, age):
    position = pos_vel[0:3]
    velocity = pos_vel[3:6]
    accel = acc_jerk[0:3]
    jolt = acc_jerk[3:6]
    step_len = age[None, :]
    new_pos = position + step_len * (velocity + step_len * (accel * 0.5 + step_len * jolt / 6.0))
    new_vel = velocity + step_len * (accel + step_len * jolt * 0.5)
    return jnp.concatenate([new_pos, new_vel], axis=0)


def pair_terms(targets, sources, masses):
    delta_pos = sources[0:3, :, None] - targets[0:3, None, :]
    delta_vel = sources[3:6, :, None] - targets[3:6, None, :]
    dist_sq = jnp.sum(delta_pos * delta_pos, axis=0) + soften
    inverse = lax.rsqrt(dist_sq)
    inv_sq = inverse * inverse
    weighted = masses[:, None] * inverse
    weighted_cube = weighted * inv_sq
    radial = 3.0 * jnp.sum(delta_pos * delta_vel, axis=0) * inv_sq
    accel = jnp.sum(weighted_cube[None] * delta_pos, axis=1)
    jolt = jnp.sum(weighted_cube[None] * (delta_vel - radial[None] * delta_pos), axis=1)
    potential = -jnp.sum(weighted, axis=0)
    return jnp.concatenate([accel, jolt, potential[None]], axis=0)


def block_terms(targets, sources, masses):
    count = targets.shape[1]
    width = min(512, count)
    nblocks = count // width
    src_count = sources.shape[1]
    src_width = min(512, src_count)
    src_blocks = src_count // src_width
    source_pieces = sources.reshape(6, src_blocks, src_width).transpose(1, 0, 2)
    mass_pieces = masses.reshape(src_blocks, src_width)
    pieces = targets.reshape(6, nblocks, width).transpose(1, 0, 2)

    def one_block(piece):

        def accumulate(total, parts):
            return (total + pair_terms(piece, parts[0], parts[1]), None)

        total, unused = lax.scan(
            accumulate, jnp.zeros((7, width), jnp.float32), (source_pieces, mass_pieces)
        )
        return total

    results = lax.map(one_block, pieces)
    return results.transpose(1, 0, 2).reshape(7, count)


def correct(history, forces):
    pred_pos = history[0:3]
    pred_vel = history[3:6]
    old_acc = history[6:9]
    old_jolt = history[9:12]
    step_len = history[12:13]
    new_acc = forces[0:3]
    new_jolt = forces[3:6]
    differ = old_acc - new_acc
    square = step_len * step_len
    cubed = square * step_len
    fourth = square * square
    fifth = fourth * step_len
    second = (-6.0 * differ - step_len * (4.0 * old_jolt + 2.0 * new_jolt)) / square
    third = (12.0 * differ + 6.0 * step_len * (old_jolt + new_jolt)) / cubed
    position = pred_pos + fourth / 24.0 * second + fifth / 120.0 * third
    velocity = pred_vel + cubed / 6.0 * second + fourth / 24.0 * third
    return jnp.concatenate([position, velocity], axis=0)


def local(pos_vel, acc_jerk, mass, age, active_local, active_owner):
    shard_rank = lax.axis_index("ja")
    predicted = predict(pos_vel, acc_jerk, age)
    stacked = jnp.concatenate([predicted, acc_jerk, age[None, :]], axis=0)
    picked = jnp.take(stacked, active_local, axis=1)
    owned = active_owner == shard_rank
    contrib = jnp.where(owned[None, :], picked, 0.0)
    history = lax.psum(contrib, "ja")
    partial_value = block_terms(history[0:6], predicted, mass)
    forces = lax.psum(partial_value, "ja")
    state = correct(history, forces)
    return (state, forces)


def solution(mesh):
    return jax.shard_map(
        local,
        mesh=mesh,
        in_specs=(
            P(None, ("grp", "ja")),
            P(None, ("grp", "ja")),
            P(("grp", "ja")),
            P(("grp", "ja")),
            P(("grp", "ia")),
            P(("grp", "ia")),
        ),
        out_specs=(P(None, ("grp", "ia")), P(None, ("grp", "ia"))),
        check_vma=False,
    )
```

profile of v0, /device:TPU:0, one launch (start us, length us, event | category | flops | bytes accessed | tf_op | source)
XLA Modules:
  0.0 92.8 jit_solution(16712219660879244907)
XLA Ops:
  7.2 0.7 compare_select_fusion
  7.9 0.9 multiply_add_fusion.1
  8.8 0.8 pad_maximum_fusion
  9.9 2.6 %gather_fusion = f32[1536,13]{1,0:T(8,128)S(1)} fusion(f32[13,1024]{0,1:T(8,128)S(1)} %copy.93, s32[2048]{0:T(1024)S(1)} %pad_clamp_fusion), kind=kCustom, calls=%fused_computation | custom fusion | bytes 165888 | tf_op jit(solution)/shard_map/jit(_take)/gather | solution.py:84
  12.8 0.7 select_bitcast_fusion
  13.5 37.3 %all-reduce.2.cloned.1.call-done = f32[13,1536]{1,0:T(8,128)} async-done(((f32[13,1536]{1,0:T(8,128)}), f32[13,1536]{1,0:T(8,128)}) %all-reduce.2.cloned.1.call-update) | async-done | bytes 79888 | tf_op jit(solution)/shard_map/psum | solution.py:87
  50.8 0.8 slice.71
  51.6 15.3 %while.22 = (s32[]{:T(128)}, f32[3,7,512]{2,1,0:T(8,128)S(1)}, f32[3,6,512]{2,1,0:T(8,128)S(1)}, f32[2,512]{1,0:T(2,128)S(1)}, f32[2,6,512]{2,1,0:T(8,128)S(1)},...) while((s32[]{:T(128)}, f32[3,7,512]{2,1,0:T(8,128)S(1)}, f32[3,6,512]{2,1,0:T(8,128)S(1)}, ...), condition=%wide.region_9.10_spmd, body=%wide.region_1.9_spmd.sunk | while | flops 12332038 | bytes 8612156 | solution.py:56
  51.6 5.1 %while.23 = (s32[]{:T(128)}, f32[7,512]{1,0:T(8,128)S(1)}, f32[2,512]{1,0:T(2,128)S(1)}, f32[2,6,512]{2,1,0:T(8,128)S(1)}, f32[6,512]{1,0:T(8,128)S(1)}, /*index=5*/s32[]{:T(128)}, s32[]{:T(128)}, s32[]{}) while((s32[]{:T(128)}, f32[7,512]{1,0:T(8,128)S(1)}, f32[2,512]{1,0:T(2,128)S(1)}, f32[2,6,512]{2,1,0:T(8,128)S(1)}, ...), condition=%wide.region_8.8_spmd.clone, body=%wide.region_2.7_spmd.clone.sunk | while | flops 12332036 | bytes 8554623 | solution.py:51
  51.7 1.0 %fusion.13 = (f32[512,512]{1,0:T(8,128)S(1)}, f32[512,512]{1,0:T(8,128)S(1)}) fusion(f32[3,512]{1,0:T(4,128)S(1)} %get-tuple-element.214, f32[3,512]{1,0:T(4,128)S(1)} %get-tuple-element.215, f32[3,512]{1,0:T(4,128)S(1)} %get-tuple-element.216, f32[3,512]{1,0:T(4,128)S(1)} %get-tuple-element.217), kind=kLoop, calls=%fused_computation.10.clone.1 | loop fusion | flops 4194304 | bytes 2121728 | tf_op jit(solution)/shard_map/while/body/eval_jaxpr/while/body/eval_jaxpr/reduce_sum | solution.py:28
  53.0 1.1 %fusion.14 = (f32[3,512]{1,0:T(4,128)S(1)}, f32[3,512]{1,0:T(4,128)S(1)}) fusion(f32[512,512]{1,0:T(8,128)S(1)} %get-tuple-element.221, f32[3,512]{1,0:T(4,128)S(1)} %get-tuple-element.216, f32[3,512]{1,0:T(4,128)S(1)} %get-tuple-element.217, f32[512,512]{1,0:T(8,128)S(1)} %get-tuple-element.222, f32[3,512]{1,0:T(4,128)S(1)} %get-tuple-element.214, ...), kind=kLoop, calls=%fused_computation.9.clone.1 | loop fusion | flops 6288384 | bytes 2134016 | tf_op jit(solution)/shard_map/while/body/eval_jaxpr/while/body/eval_jaxpr/reduce_sum | solution.py:29
  54.2 1.0 %fusion.13 = (f32[512,512]{1,0:T(8,128)S(1)}, f32[512,512]{1,0:T(8,128)S(1)}) fusion(f32[3,512]{1,0:T(4,128)S(1)} %get-tuple-element.214, f32[3,512]{1,0:T(4,128)S(1)} %get-tuple-element.215, f32[3,512]{1,0:T(4,128)S(1)} %get-tuple-element.216, f32[3,512]{1,0:T(4,128)S(1)} %get-tuple-element.217), kind=kLoop, calls=%fused_computation.10.clone.1 | loop fusion | flops 4194304 | bytes 2121728 | tf_op jit(solution)/shard_map/while/body/eval_jaxpr/while/body/eval_jaxpr/reduce_sum | solution.py:28
  55.5 1.1 %fusion.14 = (f32[3,512]{1,0:T(4,128)S(1)}, f32[3,512]{1,0:T(4,128)S(1)}) fusion(f32[512,512]{1,0:T(8,128)S(1)} %get-tuple-element.221, f32[3,512]{1,0:T(4,128)S(1)} %get-tuple-element.216, f32[3,512]{1,0:T(4,128)S(1)} %get-tuple-element.217, f32[512,512]{1,0:T(8,128)S(1)} %get-tuple-element.222, f32[3,512]{1,0:T(4,128)S(1)} %get-tuple-element.214, ...), kind=kLoop, calls=%fused_computation.9.clone.1 | loop fusion | flops 6288384 | bytes 2134016 | tf_op jit(solution)/shard_map/while/body/eval_jaxpr/while/body/eval_jaxpr/reduce_sum | solution.py:29
  56.7 5.1 %while.23 = (s32[]{:T(128)}, f32[7,512]{1,0:T(8,128)S(1)}, f32[2,512]{1,0:T(2,128)S(1)}, f32[2,6,512]{2,1,0:T(8,128)S(1)}, f32[6,512]{1,0:T(8,128)S(1)}, /*index=5*/s32[]{:T(128)}, s32[]{:T(128)}, s32[]{}) while((s32[]{:T(128)}, f32[7,512]{1,0:T(8,128)S(1)}, f32[2,512]{1,0:T(2,128)S(1)}, f32[2,6,512]{2,1,0:T(8,128)S(1)}, ...), condition=%wide.region_8.8_spmd.clone, body=%wide.region_2.7_spmd.clone.sunk | while | flops 12332036 | bytes 8554623 | solution.py:51
  56.8 1.0 %fusion.13 = (f32[512,512]{1,0:T(8,128)S(1)}, f32[512,512]{1,0:T(8,128)S(1)}) fusion(f32[3,512]{1,0:T(4,128)S(1)} %get-tuple-element.214, f32[3,512]{1,0:T(4,128)S(1)} %get-tuple-element.215, f32[3,512]{1,0:T(4,128)S(1)} %get-tuple-element.216, f32[3,512]{1,0:T(4,128)S(1)} %get-tuple-element.217), kind=kLoop, calls=%fused_computation.10.clone.1 | loop fusion | flops 4194304 | bytes 2121728 | tf_op jit(solution)/shard_map/while/body/eval_jaxpr/while/body/eval_jaxpr/reduce_sum | solution.py:28
  58.1 1.1 %fusion.14 = (f32[3,512]{1,0:T(4,128)S(1)}, f32[3,512]{1,0:T(4,128)S(1)}) fusion(f32[512,512]{1,0:T(8,128)S(1)} %get-tuple-element.221, f32[3,512]{1,0:T(4,128)S(1)} %get-tuple-element.216, f32[3,512]{1,0:T(4,128)S(1)} %get-tuple-element.217, f32[512,512]{1,0:T(8,128)S(1)} %get-tuple-element.222, f32[3,512]{1,0:T(4,128)S(1)} %get-tuple-element.214, ...), kind=kLoop, calls=%fused_computation.9.clone.1 | loop fusion | flops 6288384 | bytes 2134016 | tf_op jit(solution)/shard_map/while/body/eval_jaxpr/while/body/eval_jaxpr/reduce_sum | solution.py:29
  59.3 1.0 %fusion.13 = (f32[512,512]{1,0:T(8,128)S(1)}, f32[512,512]{1,0:T(8,128)S(1)}) fusion(f32[3,512]{1,0:T(4,128)S(1)} %get-tuple-element.214, f32[3,512]{1,0:T(4,128)S(1)} %get-tuple-element.215, f32[3,512]{1,0:T(4,128)S(1)} %get-tuple-element.216, f32[3,512]{1,0:T(4,128)S(1)} %get-tuple-element.217), kind=kLoop, calls=%fused_computation.10.clone.1 | loop fusion | flops 4194304 | bytes 2121728 | tf_op jit(solution)/shard_map/while/body/eval_jaxpr/while/body/eval_jaxpr/reduce_sum | solution.py:28
  60.6 1.1 %fusion.14 = (f32[3,512]{1,0:T(4,128)S(1)}, f32[3,512]{1,0:T(4,128)S(1)}) fusion(f32[512,512]{1,0:T(8,128)S(1)} %get-tuple-element.221, f32[3,512]{1,0:T(4,128)S(1)} %get-tuple-element.216, f32[3,512]{1,0:T(4,128)S(1)} %get-tuple-element.217, f32[512,512]{1,0:T(8,128)S(1)} %get-tuple-element.222, f32[3,512]{1,0:T(4,128)S(1)} %get-tuple-element.214, ...), kind=kLoop, calls=%fused_computation.9.clone.1 | loop fusion | flops 6288384 | bytes 2134016 | tf_op jit(solution)/shard_map/while/body/eval_jaxpr/while/body/eval_jaxpr/reduce_sum | solution.py:29
  61.8 5.1 %while.23 = (s32[]{:T(128)}, f32[7,512]{1,0:T(8,128)S(1)}, f32[2,512]{1,0:T(2,128)S(1)}, f32[2,6,512]{2,1,0:T(8,128)S(1)}, f32[6,512]{1,0:T(8,128)S(1)}, /*index=5*/s32[]{:T(128)}, s32[]{:T(128)}, s32[]{}) while((s32[]{:T(128)}, f32[7,512]{1,0:T(8,128)S(1)}, f32[2,512]{1,0:T(2,128)S(1)}, f32[2,6,512]{2,1,0:T(8,128)S(1)}, ...), condition=%wide.region_8.8_spmd.clone, body=%wide.region_2.7_spmd.clone.sunk | while | flops 12332036 | bytes 8554623 | solution.py:51
  61.9 1.0 %fusion.13 = (f32[512,512]{1,0:T(8,128)S(1)}, f32[512,512]{1,0:T(8,128)S(1)}) fusion(f32[3,512]{1,0:T(4,128)S(1)} %get-tuple-element.214, f32[3,512]{1,0:T(4,128)S(1)} %get-tuple-element.215, f32[3,512]{1,0:T(4,128)S(1)} %get-tuple-element.216, f32[3,512]{1,0:T(4,128)S(1)} %get-tuple-element.217), kind=kLoop, calls=%fused_computation.10.clone.1 | loop fusion | flops 4194304 | bytes 2121728 | tf_op jit(solution)/shard_map/while/body/eval_jaxpr/while/body/eval_jaxpr/reduce_sum | solution.py:28
  63.2 1.1 %fusion.14 = (f32[3,512]{1,0:T(4,128)S(1)}, f32[3,512]{1,0:T(4,128)S(1)}) fusion(f32[512,512]{1,0:T(8,128)S(1)} %get-tuple-element.221, f32[3,512]{1,0:T(4,128)S(1)} %get-tuple-element.216, f32[3,512]{1,0:T(4,128)S(1)} %get-tuple-element.217, f32[512,512]{1,0:T(8,128)S(1)} %get-tuple-element.222, f32[3,512]{1,0:T(4,128)S(1)} %get-tuple-element.214, ...), kind=kLoop, calls=%fused_computation.9.clone.1 | loop fusion | flops 6288384 | bytes 2134016 | tf_op jit(solution)/shard_map/while/body/eval_jaxpr/while/body/eval_jaxpr/reduce_sum | solution.py:29
  64.4 1.0 %fusion.13 = (f32[512,512]{1,0:T(8,128)S(1)}, f32[512,512]{1,0:T(8,128)S(1)}) fusion(f32[3,512]{1,0:T(4,128)S(1)} %get-tuple-element.214, f32[3,512]{1,0:T(4,128)S(1)} %get-tuple-element.215, f32[3,512]{1,0:T(4,128)S(1)} %get-tuple-element.216, f32[3,512]{1,0:T(4,128)S(1)} %get-tuple-element.217), kind=kLoop, calls=%fused_computation.10.clone.1 | loop fusion | flops 4194304 | bytes 2121728 | tf_op jit(solution)/shard_map/while/body/eval_jaxpr/while/body/eval_jaxpr/reduce_sum | solution.py:28
  65.7 1.1 %fusion.14 = (f32[3,512]{1,0:T(4,128)S(1)}, f32[3,512]{1,0:T(4,128)S(1)}) fusion(f32[512,512]{1,0:T(8,128)S(1)} %get-tuple-element.221, f32[3,512]{1,0:T(4,128)S(1)} %get-tuple-element.216, f32[3,512]{1,0:T(4,128)S(1)} %get-tuple-element.217, f32[512,512]{1,0:T(8,128)S(1)} %get-tuple-element.222, f32[3,512]{1,0:T(4,128)S(1)} %get-tuple-element.214, ...), kind=kLoop, calls=%fused_computation.9.clone.1 | loop fusion | flops 6288384 | bytes 2134016 | tf_op jit(solution)/shard_map/while/body/eval_jaxpr/while/body/eval_jaxpr/reduce_sum | solution.py:29
  66.9 18.2 %psum.15 = f32[7,1536]{1,0:T(8,128)S(1)} all-reduce(f32[7,1536]{1,0:T(8,128)S(1)} %bitcast.36), channel_id=1, replica_groups=mesh['grp'=2,'ja'=4,'ia'=4] {'ja'}, use_global_device_ids=true, to_apply=%region_10.11 | all-reduce | flops 10752 | bytes 86016 | tf_op jit(solution)/shard_map/psum | solution.py:89
  (68 shorter events, 3.6 us)
Async XLA Ops:
  7.2 43.6 %all-reduce.2.cloned.1.call-start = ((), (), s32[]{:S(2)}) async-start(), calls=%async_computation | async-start | bytes 196608 | tf_op jit(solution)/shard_map/psum | solution.py:87
  9.6 3.1 %copy-start.2 = (s32[1536]{0:T(1024)S(1)}, s32[1536]{0:T(1024)}, u32[]{:S(2)}) copy-start(s32[1536]{0:T(1024)} %param.14) | copy-start | bytes 18436
  9.6 3.1 %copy-start.3 = (s32[1536]{0:T(1024)S(1)}, s32[1536]{0:T(1024)}, u32[]{:S(2)}) copy-start(s32[1536]{0:T(1024)} %param.15) | copy-start | bytes 18436
  9.8 3.6 %copy-start.4 = (f32[1024]{0:T(1024)S(1)}, f32[1024]{0:T(1024)}, u32[]{:S(2)}) copy-start(f32[1024]{0:T(1024)} %param.12) | copy-start | bytes 12292
  51.6 33.5 %copy-start = (f32[13,1536]{1,0:T(8,128)S(1)}, f32[13,1536]{1,0:T(8,128)}, u32[]{:S(2)}) copy-start(f32[13,1536]{1,0:T(8,128)} %all-reduce.2.cloned.1.call-done) | copy-start | bytes 239620
  85.1 0.9 copy-start.1
Sparse Core Ops, SparseCore 0:
  13.5 37.1 all-reduce.1
where the time goes:
time: 93.2 us; the launch traced here: 92.8 us
  waiting for transfers between devices  37.3 us (40%)
  other arithmetic  18.5 us (20%)
  blocking collectives  18.2 us (20%)
  between operations  14.2 us (15%)
  local copies, waits for them, and re-layouts  4.12 us (4%)
    psum x1, waiting for transfers between devices, local(): history = lax.psum(contrib, 'ja')  37.3 us
    psum x1, blocking collectives, local(): forces = lax.psum(partial_value, 'ja')  18.2 us
    reduce_sum x6, other arithmetic, pair_terms(): accel = jnp.sum(weighted_cube[None] * delta_pos, axis=1)  6.74 us
    reduce_sum x6, other arithmetic, pair_terms(): radial = 3.0 * jnp.sum(delta_pos * delta_vel, axis=0) * inv_sq  5.85 us
    gather x2, local copies, waits for them, and re-layouts, local(): picked = jnp.take(stacked, active_local, axis=1)  2.86 us
  transfers between devices with their start and end apart: 1, of which 1 were waited for; matrix products, arithmetic and copies ran while one was open for 0% of the time, Pallas kernels for 0%

commit v1 on v0

--- a/solution.py
+++ b/solution.py
@@ -86,7 +86,7 @@
     contrib = jnp.where(owned[None, :], picked, 0.0)
     history = lax.psum(contrib, "ja")
     partial_value = block_terms(history[0:6], predicted, mass)
-    forces = lax.psum(partial_value, "ja")
+    forces = jnp.sum(lax.all_gather(partial_value, "ja"), axis=0)
     state = correct(history, forces)
     return (state, forces)
 

time: 93.2 us -> 89 us (0.955)
  blocking collectives: 18.2 us -> 14 us
    psum x1 -> x0, blocking collectives: 18.2 us -> none  [local(): forces = lax.psum(partial_value, 'ja')]
    all_gather x0 -> x1, blocking collectives: none -> 14 us  [local(): forces = jnp.sum(lax.all_gather(partial_value, 'ja'), axis=0)]
where the time goes in v1:
time: 89 us; the launch traced here: 88.6 us
  waiting for transfers between devices  37.3 us (42%)
  other arithmetic  18.5 us (21%)
  between operations  14.2 us (16%)
  blocking collectives  14 us (16%)
  local copies, waits for them, and re-layouts  4.12 us (5%)
    psum x1, waiting for transfers between devices, local(): history = lax.psum(contrib, 'ja')  37.3 us
    all_gather x1, blocking collectives, local(): forces = jnp.sum(lax.all_gather(partial_value, 'ja'), axis=0)  14 us
    reduce_sum x6, other arithmetic, pair_terms(): accel = jnp.sum(weighted_cube[None] * delta_pos, axis=1)  6.74 us
    reduce_sum x6, other arithmetic, pair_terms(): radial = 3.0 * jnp.sum(delta_pos * delta_vel, axis=0) * inv_sq  5.85 us
    gather x2, local copies, waits for them, and re-layouts, local(): picked = jnp.take(stacked, active_local, axis=1)  2.86 us
    mul x6, other arithmetic, pair_terms(): weighted_cube = weighted * inv_sq  1.86 us
  transfers between devices with their start and end apart: 1, of which 1 were waited for; matrix products, arithmetic and copies ran while one was open for 0% of the time, Pallas kernels for 0%

profile of v1, /device:TPU:0, one launch (start us, length us, event | category | flops | bytes accessed | tf_op | source)
XLA Modules:
  0.0 88.6 jit_solution(1240960630054169977)
XLA Ops:
  7.2 0.7 compare_select_fusion
  7.9 0.9 multiply_add_fusion.1
  8.8 0.8 pad_maximum_fusion
  9.9 2.6 %gather_fusion = f32[1536,13]{1,0:T(8,128)S(1)} fusion(f32[13,1024]{0,1:T(8,128)S(1)} %copy.109, s32[2048]{0:T(1024)S(1)} %pad_clamp_fusion), kind=kCustom, calls=%fused_computation | custom fusion | bytes 165888 | tf_op jit(solution)/shard_map/jit(_take)/gather | solution.py:84
  12.8 0.7 select_bitcast_fusion
  13.5 37.3 %all-reduce.2.cloned.1.call-done = f32[13,1536]{1,0:T(8,128)} async-done(((f32[13,1536]{1,0:T(8,128)}), f32[13,1536]{1,0:T(8,128)}) %all-reduce.2.cloned.1.call-update) | async-done | bytes 79888 | tf_op jit(solution)/shard_map/psum | solution.py:87
  50.8 0.8 slice.71
  51.6 15.3 %while.22 = (s32[]{:T(128)}, f32[3,7,512]{2,1,0:T(8,128)S(1)}, f32[3,6,512]{2,1,0:T(8,128)S(1)}, f32[2,512]{1,0:T(2,128)S(1)}, f32[2,6,512]{2,1,0:T(8,128)S(1)},...) while((s32[]{:T(128)}, f32[3,7,512]{2,1,0:T(8,128)S(1)}, f32[3,6,512]{2,1,0:T(8,128)S(1)}, ...), condition=%wide.region_9.10_spmd, body=%wide.region_1.9_spmd.sunk | while | flops 12332038 | bytes 8612156 | solution.py:56
  51.6 5.1 %while.23 = (s32[]{:T(128)}, f32[7,512]{1,0:T(8,128)S(1)}, f32[2,512]{1,0:T(2,128)S(1)}, f32[2,6,512]{2,1,0:T(8,128)S(1)}, f32[6,512]{1,0:T(8,128)S(1)}, /*index=5*/s32[]{:T(128)}, s32[]{:T(128)}, s32[]{}) while((s32[]{:T(128)}, f32[7,512]{1,0:T(8,128)S(1)}, f32[2,512]{1,0:T(2,128)S(1)}, f32[2,6,512]{2,1,0:T(8,128)S(1)}, ...), condition=%wide.region_8.8_spmd.clone, body=%wide.region_2.7_spmd.clone.sunk | while | flops 12332036 | bytes 8554623 | solution.py:51
  51.7 1.0 %fusion.13 = (f32[512,512]{1,0:T(8,128)S(1)}, f32[512,512]{1,0:T(8,128)S(1)}) fusion(f32[3,512]{1,0:T(4,128)S(1)} %get-tuple-element.212, f32[3,512]{1,0:T(4,128)S(1)} %get-tuple-element.213, f32[3,512]{1,0:T(4,128)S(1)} %get-tuple-element.214, f32[3,512]{1,0:T(4,128)S(1)} %get-tuple-element.215), kind=kLoop, calls=%fused_computation.10.clone.1 | loop fusion | flops 4194304 | bytes 2121728 | tf_op jit(solution)/shard_map/while/body/eval_jaxpr/while/body/eval_jaxpr/reduce_sum | solution.py:28
  53.0 1.1 %fusion.14 = (f32[3,512]{1,0:T(4,128)S(1)}, f32[3,512]{1,0:T(4,128)S(1)}) fusion(f32[512,512]{1,0:T(8,128)S(1)} %get-tuple-element.219, f32[3,512]{1,0:T(4,128)S(1)} %get-tuple-element.214, f32[3,512]{1,0:T(4,128)S(1)} %get-tuple-element.215, f32[512,512]{1,0:T(8,128)S(1)} %get-tuple-element.220, f32[3,512]{1,0:T(4,128)S(1)} %get-tuple-element.212, ...), kind=kLoop, calls=%fused_computation.9.clone.1 | loop fusion | flops 6288384 | bytes 2134016 | tf_op jit(solution)/shard_map/while/body/eval_jaxpr/while/body/eval_jaxpr/reduce_sum | solution.py:29
  54.2 1.0 %fusion.13 = (f32[512,512]{1,0:T(8,128)S(1)}, f32[512,512]{1,0:T(8,128)S(1)}) fusion(f32[3,512]{1,0:T(4,128)S(1)} %get-tuple-element.212, f32[3,512]{1,0:T(4,128)S(1)} %get-tuple-element.213, f32[3,512]{1,0:T(4,128)S(1)} %get-tuple-element.214, f32[3,512]{1,0:T(4,128)S(1)} %get-tuple-element.215), kind=kLoop, calls=%fused_computation.10.clone.1 | loop fusion | flops 4194304 | bytes 2121728 | tf_op jit(solution)/shard_map/while/body/eval_jaxpr/while/body/eval_jaxpr/reduce_sum | solution.py:28
  55.5 1.1 %fusion.14 = (f32[3,512]{1,0:T(4,128)S(1)}, f32[3,512]{1,0:T(4,128)S(1)}) fusion(f32[512,512]{1,0:T(8,128)S(1)} %get-tuple-element.219, f32[3,512]{1,0:T(4,128)S(1)} %get-tuple-element.214, f32[3,512]{1,0:T(4,128)S(1)} %get-tuple-element.215, f32[512,512]{1,0:T(8,128)S(1)} %get-tuple-element.220, f32[3,512]{1,0:T(4,128)S(1)} %get-tuple-element.212, ...), kind=kLoop, calls=%fused_computation.9.clone.1 | loop fusion | flops 6288384 | bytes 2134016 | tf_op jit(solution)/shard_map/while/body/eval_jaxpr/while/body/eval_jaxpr/reduce_sum | solution.py:29
  56.7 5.1 %while.23 = (s32[]{:T(128)}, f32[7,512]{1,0:T(8,128)S(1)}, f32[2,512]{1,0:T(2,128)S(1)}, f32[2,6,512]{2,1,0:T(8,128)S(1)}, f32[6,512]{1,0:T(8,128)S(1)}, /*index=5*/s32[]{:T(128)}, s32[]{:T(128)}, s32[]{}) while((s32[]{:T(128)}, f32[7,512]{1,0:T(8,128)S(1)}, f32[2,512]{1,0:T(2,128)S(1)}, f32[2,6,512]{2,1,0:T(8,128)S(1)}, ...), condition=%wide.region_8.8_spmd.clone, body=%wide.region_2.7_spmd.clone.sunk | while | flops 12332036 | bytes 8554623 | solution.py:51
  56.8 1.0 %fusion.13 = (f32[512,512]{1,0:T(8,128)S(1)}, f32[512,512]{1,0:T(8,128)S(1)}) fusion(f32[3,512]{1,0:T(4,128)S(1)} %get-tuple-element.212, f32[3,512]{1,0:T(4,128)S(1)} %get-tuple-element.213, f32[3,512]{1,0:T(4,128)S(1)} %get-tuple-element.214, f32[3,512]{1,0:T(4,128)S(1)} %get-tuple-element.215), kind=kLoop, calls=%fused_computation.10.clone.1 | loop fusion | flops 4194304 | bytes 2121728 | tf_op jit(solution)/shard_map/while/body/eval_jaxpr/while/body/eval_jaxpr/reduce_sum | solution.py:28
  58.1 1.1 %fusion.14 = (f32[3,512]{1,0:T(4,128)S(1)}, f32[3,512]{1,0:T(4,128)S(1)}) fusion(f32[512,512]{1,0:T(8,128)S(1)} %get-tuple-element.219, f32[3,512]{1,0:T(4,128)S(1)} %get-tuple-element.214, f32[3,512]{1,0:T(4,128)S(1)} %get-tuple-element.215, f32[512,512]{1,0:T(8,128)S(1)} %get-tuple-element.220, f32[3,512]{1,0:T(4,128)S(1)} %get-tuple-element.212, ...), kind=kLoop, calls=%fused_computation.9.clone.1 | loop fusion | flops 6288384 | bytes 2134016 | tf_op jit(solution)/shard_map/while/body/eval_jaxpr/while/body/eval_jaxpr/reduce_sum | solution.py:29
  59.3 1.0 %fusion.13 = (f32[512,512]{1,0:T(8,128)S(1)}, f32[512,512]{1,0:T(8,128)S(1)}) fusion(f32[3,512]{1,0:T(4,128)S(1)} %get-tuple-element.212, f32[3,512]{1,0:T(4,128)S(1)} %get-tuple-element.213, f32[3,512]{1,0:T(4,128)S(1)} %get-tuple-element.214, f32[3,512]{1,0:T(4,128)S(1)} %get-tuple-element.215), kind=kLoop, calls=%fused_computation.10.clone.1 | loop fusion | flops 4194304 | bytes 2121728 | tf_op jit(solution)/shard_map/while/body/eval_jaxpr/while/body/eval_jaxpr/reduce_sum | solution.py:28
  60.6 1.1 %fusion.14 = (f32[3,512]{1,0:T(4,128)S(1)}, f32[3,512]{1,0:T(4,128)S(1)}) fusion(f32[512,512]{1,0:T(8,128)S(1)} %get-tuple-element.219, f32[3,512]{1,0:T(4,128)S(1)} %get-tuple-element.214, f32[3,512]{1,0:T(4,128)S(1)} %get-tuple-element.215, f32[512,512]{1,0:T(8,128)S(1)} %get-tuple-element.220, f32[3,512]{1,0:T(4,128)S(1)} %get-tuple-element.212, ...), kind=kLoop, calls=%fused_computation.9.clone.1 | loop fusion | flops 6288384 | bytes 2134016 | tf_op jit(solution)/shard_map/while/body/eval_jaxpr/while/body/eval_jaxpr/reduce_sum | solution.py:29
  61.8 5.1 %while.23 = (s32[]{:T(128)}, f32[7,512]{1,0:T(8,128)S(1)}, f32[2,512]{1,0:T(2,128)S(1)}, f32[2,6,512]{2,1,0:T(8,128)S(1)}, f32[6,512]{1,0:T(8,128)S(1)}, /*index=5*/s32[]{:T(128)}, s32[]{:T(128)}, s32[]{}) while((s32[]{:T(128)}, f32[7,512]{1,0:T(8,128)S(1)}, f32[2,512]{1,0:T(2,128)S(1)}, f32[2,6,512]{2,1,0:T(8,128)S(1)}, ...), condition=%wide.region_8.8_spmd.clone, body=%wide.region_2.7_spmd.clone.sunk | while | flops 12332036 | bytes 8554623 | solution.py:51
  61.9 1.0 %fusion.13 = (f32[512,512]{1,0:T(8,128)S(1)}, f32[512,512]{1,0:T(8,128)S(1)}) fusion(f32[3,512]{1,0:T(4,128)S(1)} %get-tuple-element.212, f32[3,512]{1,0:T(4,128)S(1)} %get-tuple-element.213, f32[3,512]{1,0:T(4,128)S(1)} %get-tuple-element.214, f32[3,512]{1,0:T(4,128)S(1)} %get-tuple-element.215), kind=kLoop, calls=%fused_computation.10.clone.1 | loop fusion | flops 4194304 | bytes 2121728 | tf_op jit(solution)/shard_map/while/body/eval_jaxpr/while/body/eval_jaxpr/reduce_sum | solution.py:28
  63.2 1.1 %fusion.14 = (f32[3,512]{1,0:T(4,128)S(1)}, f32[3,512]{1,0:T(4,128)S(1)}) fusion(f32[512,512]{1,0:T(8,128)S(1)} %get-tuple-element.219, f32[3,512]{1,0:T(4,128)S(1)} %get-tuple-element.214, f32[3,512]{1,0:T(4,128)S(1)} %get-tuple-element.215, f32[512,512]{1,0:T(8,128)S(1)} %get-tuple-element.220, f32[3,512]{1,0:T(4,128)S(1)} %get-tuple-element.212, ...), kind=kLoop, calls=%fused_computation.9.clone.1 | loop fusion | flops 6288384 | bytes 2134016 | tf_op jit(solution)/shard_map/while/body/eval_jaxpr/while/body/eval_jaxpr/reduce_sum | solution.py:29
  64.4 1.0 %fusion.13 = (f32[512,512]{1,0:T(8,128)S(1)}, f32[512,512]{1,0:T(8,128)S(1)}) fusion(f32[3,512]{1,0:T(4,128)S(1)} %get-tuple-element.212, f32[3,512]{1,0:T(4,128)S(1)} %get-tuple-element.213, f32[3,512]{1,0:T(4,128)S(1)} %get-tuple-element.214, f32[3,512]{1,0:T(4,128)S(1)} %get-tuple-element.215), kind=kLoop, calls=%fused_computation.10.clone.1 | loop fusion | flops 4194304 | bytes 2121728 | tf_op jit(solution)/shard_map/while/body/eval_jaxpr/while/body/eval_jaxpr/reduce_sum | solution.py:28
  65.7 1.1 %fusion.14 = (f32[3,512]{1,0:T(4,128)S(1)}, f32[3,512]{1,0:T(4,128)S(1)}) fusion(f32[512,512]{1,0:T(8,128)S(1)} %get-tuple-element.219, f32[3,512]{1,0:T(4,128)S(1)} %get-tuple-element.214, f32[3,512]{1,0:T(4,128)S(1)} %get-tuple-element.215, f32[512,512]{1,0:T(8,128)S(1)} %get-tuple-element.220, f32[3,512]{1,0:T(4,128)S(1)} %get-tuple-element.212, ...), kind=kLoop, calls=%fused_computation.9.clone.1 | loop fusion | flops 6288384 | bytes 2134016 | tf_op jit(solution)/shard_map/while/body/eval_jaxpr/while/body/eval_jaxpr/reduce_sum | solution.py:29
  66.9 14.0 %all_gather.3 = f32[4,7,1536]{2,1,0:T(8,128)S(1)} all-gather(f32[1,7,1536]{2,1,0:T(8,128)S(1)} %bitcast.36), channel_id=1, replica_groups=mesh['grp'=2,'ja'=4,'ia'=4] {'ja'}, dimensions={0}, use_global_device_ids=true | all-gather | bytes 215040 | tf_op jit(solution)/shard_map/all_gather | solution.py:89
  (69 shorter events, 3.6 us)
Async XLA Ops:
  7.2 43.6 %all-reduce.2.cloned.1.call-start = ((), (), s32[]{:S(2)}) async-start(), calls=%async_computation | async-start | bytes 196608 | tf_op jit(solution)/shard_map/psum | solution.py:87
  9.6 3.1 %copy-start.2 = (s32[1536]{0:T(1024)S(1)}, s32[1536]{0:T(1024)}, u32[]{:S(2)}) copy-start(s32[1536]{0:T(1024)} %param.14) | copy-start | bytes 18436
  9.6 3.1 %copy-start.3 = (s32[1536]{0:T(1024)S(1)}, s32[1536]{0:T(1024)}, u32[]{:S(2)}) copy-start(s32[1536]{0:T(1024)} %param.15) | copy-start | bytes 18436
  9.8 3.6 %copy-start.4 = (f32[1024]{0:T(1024)S(1)}, f32[1024]{0:T(1024)}, u32[]{:S(2)}) copy-start(f32[1024]{0:T(1024)} %param.12) | copy-start | bytes 12292
  51.6 29.3 %copy-start = (f32[13,1536]{1,0:T(8,128)S(1)}, f32[13,1536]{1,0:T(8,128)}, u32[]{:S(2)}) copy-start(f32[13,1536]{1,0:T(8,128)} %all-reduce.2.cloned.1.call-done) | copy-start | bytes 239620
  80.9 0.9 copy-start.1
Sparse Core Ops, SparseCore 0:
  13.5 37.1 all-reduce.1
